TPU v7x, 32 devices: a whole 2x2x4 slice. The times are simulated.
32 devices in a mesh: dev: 2 (over x), sa: 16 (over z, y, core).
Axes of the slice: x: 2, y: 2, z: 4, core: 2. Of those that a mesh axis runs over, the one named last changes fastest.
Arguments:
- patches: bfloat16 [8, 1024, 1152], P('dev', 'sa'), may hold values from -6 to 6
- patch_mask: int32 [8, 1024], P('dev', 'sa'), may hold values from 0 to 1, as said below
- cotangent: bfloat16 [8, 1024, 1152], P('dev', 'sa'), may hold values from -6 to 6
- w_qkv: bfloat16 [1152, 3456], P('sa', 'dev'), may hold values from -0.1875 to 0.1875
- w_out: bfloat16 [1152, 1152], P('sa', 'dev'), may hold values from -0.75 to 0.75
- w_up: bfloat16 [1152, 4304], P('sa', 'dev'), may hold values from -0.1875 to 0.1875
- w_down: bfloat16 [1152, 4304], P('sa', 'dev'), may hold values from -0.125 to 0.125
- gain_one: bfloat16 [1, 1152], P(None, 'dev'), may hold values from 0.25 to 1.75
- shift_one: bfloat16 [1, 1152], P(None, 'dev'), may hold values from -4 to 4
- gain_two: bfloat16 [1, 1152], P(None, 'dev'), may hold values from 0.25 to 1.75
- shift_two: bfloat16 [1, 1152], P(None, 'dev'), may hold values from -4 to 4
- bias_query: bfloat16 [1, 1152], P(None, 'dev'), may hold values from -4 to 4
- bias_value: bfloat16 [1, 1152], P(None, 'dev'), may hold values from -4 to 4
- bias_out: bfloat16 [1, 1152], P(None, 'dev'), may hold values from -4 to 4
- bias_up: bfloat16 [1, 4304], P(None, 'dev'), may hold values from -4 to 4
- bias_down: bfloat16 [1, 1152], P(None, 'dev'), may hold values from -4 to 4
Outputs:
- result: bfloat16 [8, 1024, 1152], P('dev', 'sa')
- grad_patches: bfloat16 [8, 1024, 1152], P('dev', 'sa')
- grad_w_qkv: float32 [1152, 3456], P('sa', 'dev')
- grad_w_out: float32 [1152, 1152], P('sa', 'dev')
- grad_w_up: float32 [1152, 4304], P('sa', 'dev')
- grad_w_down: float32 [1152, 4304], P('sa', 'dev')
- grad_gain_one: float32 [1, 1152], P(None, 'dev')
- grad_shift_one: float32 [1, 1152], P(None, 'dev')
- grad_gain_two: float32 [1, 1152], P(None, 'dev')
- grad_shift_two: float32 [1, 1152], P(None, 'dev')
- grad_bias_query: float32 [1, 1152], P(None, 'dev')
- grad_bias_value: float32 [1, 1152], P(None, 'dev')
- grad_bias_out: float32 [1, 1152], P(None, 'dev')
- grad_bias_up: float32 [1, 4304], P(None, 'dev')
- grad_bias_down: float32 [1, 1152], P(None, 'dev')
Inputs may be any that keep to these rules, and one draw needn't show every extreme that they name: `patch_mask`: each image's ones are its first patches, 256 of them or more.
All inputs are finite; a program needn't handle non-finite values.
Results may differ from a plain program's by a relative error of at most 0.018.
Values may be sent and summed in bfloat16 or wider, within the bound.
No kernel may reach another device: no remote copies, remote signals or barrier semaphores. Data moves between devices by JAX's collectives and lax.ppermute only.
A program may use at most 256 MiB of HBM per device.

v0:
```python
import jax
import jax.numpy as jnp
from jax import lax
from jax.sharding import PartitionSpec as P

HEADS = 16
HEAD_DIM = 72
MICRO = 4


def normalize(values, gain, shift):
    centre = values - jnp.mean(values, axis=-1, keepdims=True)
    spread = jnp.mean(centre * centre, axis=-1, keepdims=True)
    return centre * lax.rsqrt(spread + 1e-06) * gain + shift


def gelu_tanh(values):
    return jax.nn.gelu(values, approximate=True)


def mat_rows(left, right):
    return lax.dot_general(
        left, right, (((0,), (0,)), ((), ())), preferred_element_type=jnp.float32
    )


def mat_last(left, right):
    return lax.dot_general(
        left, right, (((1,), (1,)), ((), ())), preferred_element_type=jnp.float32
    )


def score_block(query, all_kv, all_valid, width):
    images = all_kv.shape[0]
    seq_len = all_kv.shape[1]
    q_heads = query.reshape(images, -1, HEADS, HEAD_DIM)
    key_heads = all_kv[:, :, :width].reshape(images, seq_len, HEADS, HEAD_DIM)
    raw = jnp.einsum("iqhd,ikhd->ihqk", q_heads, key_heads, preferred_element_type=jnp.float32)
    raw = raw * HEAD_DIM ** (-0.5)
    return jnp.where(all_valid[:, None, None, :] > 0.5, raw, -1e30)


def per_device(
    patches,
    patch_mask,
    cotangent,
    w_qkv,
    w_out,
    w_up,
    w_down,
    gain_one,
    shift_one,
    gain_two,
    shift_two,
    bias_query,
    bias_value,
    bias_out,
    bias_up,
    bias_down,
):
    width = patches.shape[2]
    local_tokens = patches.shape[1]
    per_micro = patches.shape[0] // MICRO
    row_count = per_micro * local_tokens
    scale = HEAD_DIM ** (-0.5)
    row_parts = (
        lax.all_gather(w_qkv, "sa", axis=0, tiled=True),
        lax.all_gather(w_out, "sa", axis=0, tiled=True),
        lax.all_gather(w_up, "sa", axis=0, tiled=True),
        lax.all_gather(w_down, "sa", axis=0, tiled=True),
    )
    gathered = (
        lax.all_gather(row_parts[0], "dev", axis=1, tiled=True),
        lax.all_gather(row_parts[1], "dev", axis=1, tiled=True),
        lax.all_gather(row_parts[2], "dev", axis=1, tiled=True),
        lax.all_gather(row_parts[3], "dev", axis=1, tiled=True),
        lax.all_gather(gain_one, "dev", axis=1, tiled=True),
        lax.all_gather(shift_one, "dev", axis=1, tiled=True),
        lax.all_gather(gain_two, "dev", axis=1, tiled=True),
        lax.all_gather(shift_two, "dev", axis=1, tiled=True),
        lax.all_gather(bias_query, "dev", axis=1, tiled=True),
        lax.all_gather(bias_value, "dev", axis=1, tiled=True),
        lax.all_gather(bias_out, "dev", axis=1, tiled=True),
        lax.all_gather(bias_up, "dev", axis=1, tiled=True),
        lax.all_gather(bias_down, "dev", axis=1, tiled=True),
    )
    full_qkv, full_out, full_up, full_down = (gathered[0], gathered[1], gathered[2], gathered[3])
    vectors = [item.astype(jnp.float32)[0] for item in gathered[4:]]
    gain_first, shift_first, gain_second, shift_second = (
        vectors[0],
        vectors[1],
        vectors[2],
        vectors[3],
    )
    query_bias, value_bias, out_bias, up_bias, down_bias = (
        vectors[4],
        vectors[5],
        vectors[6],
        vectors[7],
        vectors[8],
    )
    qkv_bias = jnp.concatenate([query_bias, jnp.zeros((width,), jnp.float32), value_bias])
    outputs = []
    kept = []
    for micro_step in range(MICRO):
        begin = micro_step * per_micro
        inputs = patches[begin : begin + per_micro].astype(jnp.float32).reshape(row_count, width)
        normed_one = normalize(inputs, gain_first, shift_first).astype(jnp.bfloat16)
        projected = (
            jnp.dot(normed_one, full_qkv, preferred_element_type=jnp.float32) + qkv_bias
        ).astype(jnp.bfloat16)
        query = projected[:, :width]
        key_value = projected[:, width:].reshape(per_micro, local_tokens, 2 * width)
        valid = patch_mask[begin : begin + per_micro].astype(jnp.bfloat16)
        all_kv, all_valid = (
            lax.all_gather(key_value, "sa", axis=1, tiled=True),
            lax.all_gather(valid, "sa", axis=1, tiled=True),
        )
        seq_len = all_kv.shape[1]
        scores = score_block(query, all_kv, all_valid, width)
        peak = jnp.max(scores, axis=-1, keepdims=True)
        expo = jnp.exp(scores - peak)
        total = jnp.sum(expo, axis=-1, keepdims=True)
        log_total = peak + jnp.log(total)
        probs = (expo / total).astype(jnp.bfloat16)
        value_heads = all_kv[:, :, width:].reshape(per_micro, seq_len, HEADS, HEAD_DIM)
        attended = jnp.einsum(
            "ihqk,ikhd->iqhd", probs, value_heads, preferred_element_type=jnp.float32
        )
        attended = attended.reshape(row_count, width).astype(jnp.bfloat16)
        middle = inputs + jnp.dot(attended, full_out, preferred_element_type=jnp.float32) + out_bias
        normed_two = normalize(middle, gain_second, shift_second).astype(jnp.bfloat16)
        hidden_pre = jnp.dot(normed_two, full_up, preferred_element_type=jnp.float32) + up_bias
        activated = gelu_tanh(hidden_pre).astype(jnp.bfloat16)
        mlp_out = mat_last(activated, full_down) + down_bias
        outputs.append(
            (middle + mlp_out).astype(jnp.bfloat16).reshape(per_micro, local_tokens, width)
        )
        kept.append(
            (
                inputs,
                normed_one,
                query,
                key_value,
                valid,
                all_kv,
                all_valid,
                log_total,
                attended,
                middle,
                normed_two,
                hidden_pre,
                activated,
            )
        )
    rows_back = (
        lax.all_gather(w_qkv, "sa", axis=0, tiled=True),
        lax.all_gather(w_out, "sa", axis=0, tiled=True),
        lax.all_gather(w_up, "sa", axis=0, tiled=True),
        lax.all_gather(w_down, "sa", axis=0, tiled=True),
    )
    again = (
        lax.all_gather(rows_back[0], "dev", axis=1, tiled=True),
        lax.all_gather(rows_back[1], "dev", axis=1, tiled=True),
        lax.all_gather(rows_back[2], "dev", axis=1, tiled=True),
        lax.all_gather(rows_back[3], "dev", axis=1, tiled=True),
        lax.all_gather(gain_one, "dev", axis=1, tiled=True),
        lax.all_gather(shift_one, "dev", axis=1, tiled=True),
        lax.all_gather(gain_two, "dev", axis=1, tiled=True),
        lax.all_gather(shift_two, "dev", axis=1, tiled=True),
        lax.all_gather(bias_query, "dev", axis=1, tiled=True),
        lax.all_gather(bias_value, "dev", axis=1, tiled=True),
        lax.all_gather(bias_out, "dev", axis=1, tiled=True),
        lax.all_gather(bias_up, "dev", axis=1, tiled=True),
        lax.all_gather(bias_down, "dev", axis=1, tiled=True),
    )
    back_qkv, back_out, back_up, back_down = (again[0], again[1], again[2], again[3])
    back_vectors = [item.astype(jnp.float32)[0] for item in again[4:]]
    back_gain_first, back_shift_first = (back_vectors[0], back_vectors[1])
    back_gain_second, back_shift_second = (back_vectors[2], back_vectors[3])
    acc_qkv = jnp.zeros(back_qkv.shape, jnp.float32)
    acc_out = jnp.zeros(back_out.shape, jnp.float32)
    acc_up = jnp.zeros(back_up.shape, jnp.float32)
    acc_down = jnp.zeros(back_down.shape, jnp.float32)
    ff_width = back_up.shape[1]
    acc_vectors = [jnp.zeros((width,), jnp.float32) for index_value in range(7)] + [
        jnp.zeros((ff_width,), jnp.float32),
        jnp.zeros((width,), jnp.float32),
    ]
    grad_inputs = []
    for micro_step in range(MICRO):
        begin = micro_step * per_micro
        (
            inputs,
            normed_one,
            query,
            key_value,
            valid,
            all_kv,
            all_valid,
            log_total,
            attended,
            middle,
            normed_two,
            hidden_pre,
            activated,
        ) = kept[micro_step]
        seq_len = all_kv.shape[1]
        grad_out = (
            cotangent[begin : begin + per_micro].astype(jnp.float32).reshape(row_count, width)
        )
        grad_mlp = grad_out.astype(jnp.bfloat16)
        acc_down = acc_down + mat_rows(grad_mlp, activated)
        grad_act = jnp.dot(grad_mlp, back_down, preferred_element_type=jnp.float32)
        gelu_pull = jax.vjp(gelu_tanh, hidden_pre)[1]
        grad_hidden = gelu_pull(grad_act)[0].astype(jnp.bfloat16)
        acc_up = acc_up + mat_rows(normed_two, grad_hidden)
        grad_normed_two = mat_last(grad_hidden, back_up)
        norm_pull = jax.vjp(normalize, middle, back_gain_second, back_shift_second)[1]
        grad_middle_part, grad_gain_second, grad_shift_second = norm_pull(grad_normed_two)
        grad_middle = grad_out + grad_middle_part
        grad_branch = grad_middle.astype(jnp.bfloat16)
        acc_out = acc_out + mat_rows(attended, grad_branch)
        grad_att = mat_last(grad_branch, back_out).astype(jnp.bfloat16)
        grad_att_heads = grad_att.reshape(per_micro, local_tokens, HEADS, HEAD_DIM)
        scores = score_block(query, all_kv, all_valid, width)
        probs_full = jnp.exp(scores - log_total)
        probs = probs_full.astype(jnp.bfloat16)
        q_heads = query.reshape(per_micro, local_tokens, HEADS, HEAD_DIM)
        key_heads = all_kv[:, :, :width].reshape(per_micro, seq_len, HEADS, HEAD_DIM)
        value_heads = all_kv[:, :, width:].reshape(per_micro, seq_len, HEADS, HEAD_DIM)
        grad_probs = jnp.einsum(
            "iqhd,ikhd->ihqk", grad_att_heads, value_heads, preferred_element_type=jnp.float32
        )
        row_terms = jnp.sum(grad_probs * probs_full, axis=-1, keepdims=True)
        grad_scores = (probs_full * (grad_probs - row_terms)).astype(jnp.bfloat16)
        grad_query = (
            jnp.einsum(
                "ihqk,ikhd->iqhd", grad_scores, key_heads, preferred_element_type=jnp.float32
            )
            * scale
        )
        grad_value = jnp.einsum(
            "ihqk,iqhd->ikhd", probs, grad_att_heads, preferred_element_type=jnp.float32
        )
        grad_key = (
            jnp.einsum("ihqk,iqhd->ikhd", grad_scores, q_heads, preferred_element_type=jnp.float32)
            * scale
        )
        grad_kv_part = jnp.concatenate(
            [
                grad_key.reshape(per_micro, seq_len, width),
                grad_value.reshape(per_micro, seq_len, width),
            ],
            axis=2,
        )
        grad_kv = lax.psum_scatter(
            grad_kv_part.astype(jnp.bfloat16), "sa", scatter_dimension=1, tiled=True
        ).astype(jnp.float32)
        grad_proj = jnp.concatenate(
            [grad_query.reshape(row_count, width), grad_kv.reshape(row_count, 2 * width)], axis=1
        ).astype(jnp.bfloat16)
        acc_qkv = acc_qkv + mat_rows(normed_one, grad_proj)
        grad_normed_one = mat_last(grad_proj, back_qkv)
        first_pull = jax.vjp(normalize, inputs, back_gain_first, back_shift_first)[1]
        grad_in_part, grad_gain_first, grad_shift_first = first_pull(grad_normed_one)
        grad_inputs.append(
            (grad_middle + grad_in_part)
            .astype(jnp.bfloat16)
            .reshape(per_micro, local_tokens, width)
        )
        proj_sums = jnp.sum(grad_proj.astype(jnp.float32), axis=0)
        terms = [
            grad_gain_first,
            grad_shift_first,
            grad_gain_second,
            grad_shift_second,
            proj_sums[:width],
            proj_sums[2 * width :],
            jnp.sum(grad_branch.astype(jnp.float32), axis=0),
            jnp.sum(grad_hidden.astype(jnp.float32), axis=0),
            jnp.sum(grad_mlp.astype(jnp.float32), axis=0),
        ]
        acc_vectors = [held + fresh for held, fresh in zip(acc_vectors, terms)]
    row_sums = (
        lax.psum_scatter(
            acc_qkv.astype(jnp.bfloat16), "sa", scatter_dimension=0, tiled=True
        ).astype(jnp.float32),
        lax.psum_scatter(
            acc_out.astype(jnp.bfloat16), "sa", scatter_dimension=0, tiled=True
        ).astype(jnp.float32),
        lax.psum_scatter(acc_up.astype(jnp.bfloat16), "sa", scatter_dimension=0, tiled=True).astype(
            jnp.float32
        ),
        lax.psum_scatter(
            acc_down.astype(jnp.bfloat16), "sa", scatter_dimension=0, tiled=True
        ).astype(jnp.float32),
    )
    flat_vectors = [item[None, :] for item in acc_vectors]
    column_sums = (
        lax.psum_scatter(
            row_sums[0].astype(jnp.bfloat16), "dev", scatter_dimension=1, tiled=True
        ).astype(jnp.float32),
        lax.psum_scatter(
            row_sums[1].astype(jnp.bfloat16), "dev", scatter_dimension=1, tiled=True
        ).astype(jnp.float32),
        lax.psum_scatter(
            row_sums[2].astype(jnp.bfloat16), "dev", scatter_dimension=1, tiled=True
        ).astype(jnp.float32),
        lax.psum_scatter(
            row_sums[3].astype(jnp.bfloat16), "dev", scatter_dimension=1, tiled=True
        ).astype(jnp.float32),
        lax.psum_scatter(
            flat_vectors[0].astype(jnp.bfloat16), "dev", scatter_dimension=1, tiled=True
        ).astype(jnp.float32),
        lax.psum_scatter(
            flat_vectors[1].astype(jnp.bfloat16), "dev", scatter_dimension=1, tiled=True
        ).astype(jnp.float32),
        lax.psum_scatter(
            flat_vectors[2].astype(jnp.bfloat16), "dev", scatter_dimension=1, tiled=True
        ).astype(jnp.float32),
        lax.psum_scatter(
            flat_vectors[3].astype(jnp.bfloat16), "dev", scatter_dimension=1, tiled=True
        ).astype(jnp.float32),
        lax.psum_scatter(
            flat_vectors[4].astype(jnp.bfloat16), "dev", scatter_dimension=1, tiled=True
        ).astype(jnp.float32),
        lax.psum_scatter(
            flat_vectors[5].astype(jnp.bfloat16), "dev", scatter_dimension=1, tiled=True
        ).astype(jnp.float32),
        lax.psum_scatter(
            flat_vectors[6].astype(jnp.bfloat16), "dev", scatter_dimension=1, tiled=True
        ).astype(jnp.float32),
        lax.psum_scatter(
            flat_vectors[7].astype(jnp.bfloat16), "dev", scatter_dimension=1, tiled=True
        ).astype(jnp.float32),
        lax.psum_scatter(
            flat_vectors[8].astype(jnp.bfloat16), "dev", scatter_dimension=1, tiled=True
        ).astype(jnp.float32),
    )
    summed = lax.psum(
        (
            column_sums[4],
            column_sums[5],
            column_sums[6],
            column_sums[7],
            column_sums[8],
            column_sums[9],
            column_sums[10],
            column_sums[11],
            column_sums[12],
        ),
        "sa",
    )
    result = jnp.concatenate(outputs, axis=0)
    grad_patches = jnp.concatenate(grad_inputs, axis=0)
    return (
        result,
        grad_patches,
        column_sums[0],
        column_sums[1],
        column_sums[2],
        column_sums[3],
        summed[0],
        summed[1],
        summed[2],
        summed[3],
        summed[4],
        summed[5],
        summed[6],
        summed[7],
        summed[8],
    )


def solution(mesh):
    placed = (
        P("dev", "sa", None),
        P("dev", "sa"),
        P("dev", "sa", None),
        P("sa", "dev"),
        P("sa", "dev"),
        P("sa", "dev"),
        P("sa", "dev"),
        P(None, "dev"),
        P(None, "dev"),
        P(None, "dev"),
        P(None, "dev"),
        P(None, "dev"),
        P(None, "dev"),
        P(None, "dev"),
        P(None, "dev"),
        P(None, "dev"),
    )
    return jax.shard_map(
        per_device,
        mesh=mesh,
        in_specs=placed,
        out_specs=(
            P("dev", "sa", None),
            P("dev", "sa", None),
            P("sa", "dev"),
            P("sa", "dev"),
            P("sa", "dev"),
            P("sa", "dev"),
            P(None, "dev"),
            P(None, "dev"),
            P(None, "dev"),
            P(None, "dev"),
            P(None, "dev"),
            P(None, "dev"),
            P(None, "dev"),
            P(None, "dev"),
            P(None, "dev"),
        ),
        check_vma=False,
    )
```

profile of v0, /device:TPU:0, one launch (start us, length us, event | category | flops | bytes accessed | tf_op | source)
XLA Modules:
  0.0 1915.4 jit_solution(13595690874956938875)
XLA Ops:
  8.0 55.3 %all-gather.17.cloned.1.call-done = bf16[1152,1728]{1,0:T(8,128)(2,1)} async-done(((bf16[72,1728]{1,0:T(8,128)(2,1)}), bf16[1152,1728]{1,0:T(8,128)(2,1)}) %all-gather.17.cloned.1.call-update) | async-done | bytes 3981328 | tf_op jit(solution)/shard_map/all_gather | solution.py:67
  75.8 8.9 all-reduce.21
  85.8 82.3 %all-gather.19.cloned.1.call-done = bf16[1152,3456]{0,1:T(8,128)(2,1)} async-done(((bf16[1152,1728]{0,1:T(8,128)(2,1)}), bf16[1152,3456]{0,1:T(8,128)(2,1)}) %all-gather.19.cloned.1.call-update) | async-done | bytes 7962640 | tf_op jit(solution)/shard_map/all_gather | solution.py:73
  188.1 21.2 %all-gather.21.cloned.1.call-done = bf16[1152,576]{1,0:T(8,128)(2,1)} async-done(((bf16[72,576]{1,0:T(8,128)(2,1)}), bf16[1152,576]{1,0:T(8,128)(2,1)}) %all-gather.21.cloned.1.call-update) | async-done | bytes 1327120 | tf_op jit(solution)/shard_map/all_gather | solution.py:68
  211.9 53.1 %all-gather.25.cloned.1.call-done = bf16[1152,2152]{1,0:T(8,128)(2,1)} async-done(((bf16[72,2152]{1,0:T(8,128)(2,1)}), bf16[1152,2152]{1,0:T(8,128)(2,1)}) %all-gather.25.cloned.1.call-update) | async-done | bytes 4958224 | tf_op jit(solution)/shard_map/all_gather | solution.py:69
  265.0 8.5 copy.148
  277.5 32.7 %all-reduce.19 = (bf16[1024]{0:T(1024)(128)(2,1)S(1)}, bf16[1024]{0:T(1024)(128)(2,1)S(1)}, bf16[1024]{0:T(1024)(128)(2,1)S(1)}, bf16[1024]{0:T(1024)(128)(2,1)S(1)}) all-reduce(bf16[1024]{0:T(1024)(128)(2,1)S(1)} %dynamic-update-slice.10, bf16[1024]{0:T(1024)(128)(2,1)S(1)} %dynamic-update-slice.12, ...), channel_id=1, replica_groups=mesh['dev'=2,'sa'=16] {'sa'}, use_global_device_ids=true, to_apply=%add.10 | all-reduce | flops 4096 | bytes 16384
  310.8 10.2 all-gather.29.cloned.1.call-done
  321.0 8.4 copy.149
  332.0 44.0 %all-gather.35.cloned.1.call-done = bf16[1024,2304]{1,0:T(8,128)(2,1)} async-done(((bf16[64,2304]{1,0:T(8,128)(2,1)}), bf16[1024,2304]{1,0:T(8,128)(2,1)}) %all-gather.35.cloned.1.call-update) | async-done | bytes 4718608 | tf_op jit(solution)/shard_map/all_gather | solution.py:116
  382.7 48.1 %all-gather.37.cloned.1.call-done = bf16[1024,2304]{1,0:T(8,128)(2,1)} async-done(((bf16[64,2304]{1,0:T(8,128)(2,1)}), bf16[1024,2304]{1,0:T(8,128)(2,1)}) %all-gather.37.cloned.1.call-update) | async-done | bytes 4718608 | tf_op jit(solution)/shard_map/all_gather | solution.py:116
  438.5 47.1 %all-gather.39.cloned.1.call-done = bf16[1024,2304]{1,0:T(8,128)(2,1)} async-done(((bf16[64,2304]{1,0:T(8,128)(2,1)}), bf16[1024,2304]{1,0:T(8,128)(2,1)}) %all-gather.39.cloned.1.call-update) | async-done | bytes 4718608 | tf_op jit(solution)/shard_map/all_gather | solution.py:116
  543.8 106.0 %all-gather.27.cloned.1.call-done = bf16[1152,4304]{0,1:T(8,128)(2,1)} async-done(((bf16[1152,2152]{0,1:T(8,128)(2,1)}), bf16[1152,4304]{0,1:T(8,128)(2,1)}) %all-gather.27.cloned.1.call-update) | async-done | bytes 9916432 | tf_op jit(solution)/shard_map/all_gather | solution.py:75
  649.9 16.5 convolution_add_fusion.14
  666.4 108.3 %all-gather.31.cloned.1.call-done = bf16[1152,4304]{0,1:T(8,128)(2,1)} async-done(((bf16[1152,2152]{0,1:T(8,128)(2,1)}), bf16[1152,4304]{0,1:T(8,128)(2,1)}) %all-gather.31.cloned.1.call-update) | async-done | bytes 9916432 | tf_op jit(solution)/shard_map/all_gather | solution.py:76
  829.9 21.4 %copy.189 = bf16[1,1024,2304]{2,0,1:T(2,128)(2,1)} copy(bf16[1,1024,2304]{1,2,0:T(8,128)(2,1)} %pad_maximum_fusion.1) | data formatting | bytes 9437184
  871.4 21.5 %copy.193 = bf16[1,1024,2304]{2,0,1:T(2,128)(2,1)} copy(bf16[1,1024,2304]{1,2,0:T(8,128)(2,1)} %pad_maximum_fusion.3) | data formatting | bytes 9437184
  912.9 21.5 %copy.191 = bf16[1,1024,2304]{2,0,1:T(2,128)(2,1)} copy(bf16[1,1024,2304]{1,2,0:T(8,128)(2,1)} %pad_maximum_fusion.2) | data formatting | bytes 9437184
  963.3 49.4 %reduce-scatter.66.cloned.1.call-done = bf16[64,2304]{1,0:T(8,128)(2,1)} async-done(((bf16[1024,2304]{1,0:T(8,128)(2,1)}), bf16[64,2304]{1,0:T(8,128)(2,1)}) %reduce-scatter.66.cloned.1.call-update) | async-done | bytes 294928
  1016.8 74.2 %reduce-scatter.64.cloned.1.call-done = bf16[64,2304]{1,0:T(8,128)(2,1)} async-done(((bf16[1024,2304]{1,0:T(8,128)(2,1)}), bf16[64,2304]{1,0:T(8,128)(2,1)}) %reduce-scatter.64.cloned.1.call-update) | async-done | bytes 294928
  1115.5 49.6 %all-gather.33.cloned.1.call-done = bf16[1024,2304]{1,0:T(8,128)(2,1)} async-done(((bf16[64,2304]{1,0:T(8,128)(2,1)}), bf16[1024,2304]{1,0:T(8,128)(2,1)}) %all-gather.33.cloned.1.call-update) | async-done | bytes 4718608 | tf_op jit(solution)/shard_map/all_gather | solution.py:116
  1225.3 21.5 %copy.187 = bf16[1,1024,2304]{2,0,1:T(2,128)(2,1)} copy(bf16[1,1024,2304]{1,2,0:T(8,128)(2,1)} %pad_maximum_fusion) | data formatting | bytes 9437184
  1255.4 8.5 fusion.245
  1264.0 12.9 convolution_add_fusion.5
  1277.0 13.4 convolution_add_fusion.4
  1290.3 13.4 fusion
  1305.4 8.4 fusion.201
  1313.9 12.6 convolution_add_fusion.2
  1328.8 12.8 convolution_add_fusion.1
  1343.4 14.0 fusion.2
  1357.5 14.1 copy.201
  1381.9 11.2 fusion.156
  1393.1 8.7 convolution_add_fusion.8
  1401.9 8.2 convolution_add_fusion.7
  1410.1 11.2 fusion.3
  1433.4 9.1 all-reduce.20
  1470.5 18.1 reduce-scatter.58.cloned.1.call-done
  1503.6 12.8 reduce-scatter.78.cloned.1.call-done
  1518.0 12.8 reduce-scatter.80.cloned.1.call-done
  1532.4 12.8 reduce-scatter.70.cloned.1.call-done
  1546.9 119.3 %reduce-scatter.72.cloned.1.call-done = bf16[72,4304]{1,0:T(8,128)(2,1)} async-done(((bf16[1152,4304]{1,0:T(8,128)(2,1)}), bf16[72,4304]{1,0:T(8,128)(2,1)}) %reduce-scatter.72.cloned.1.call-update) | async-done | bytes 619792
  1674.3 96.4 %reduce-scatter.90.cloned.1.call-done = bf16[72,3456]{1,0:T(8,128)(2,1)} async-done(((bf16[1152,3456]{1,0:T(8,128)(2,1)}), bf16[72,3456]{1,0:T(8,128)(2,1)}) %reduce-scatter.90.cloned.1.call-update) | async-done | bytes 497680
  1775.0 10.2 reduce-scatter.74.cloned.1.call-done
  1786.3 13.7 reduce-scatter.76.cloned.1.call-done
  1801.0 13.3 reduce-scatter.84.cloned.1.call-done
  1815.3 13.3 reduce-scatter.82.cloned.1.call-done
  1829.7 63.4 %all-reduce.18 = (f32[1,576]{1,0:T(1,128)}, f32[1,576]{1,0:T(1,128)}, f32[1,576]{1,0:T(1,128)}, f32[1,576]{1,0:T(1,128)}, f32[1,576]{1,0:T(1,128)}, /*index=5*/f...) all-reduce(bf16[1,576]{1,0:T(2,128)(2,1)S(1)} %copy.204, ...), channel_id=1, replica_groups=mesh['dev'=2,'sa'=16] {'sa'}, use_global_device_ids=true, to_apply=%region_61.62 | all-reduce | flops 6760 | bytes 44864 | tf_op jit(solution)/shard_map/psum | solution.py:341
  1897.2 9.2 reduce-scatter.68.cloned.1.call-done
  (836 shorter events, 431.1 us)
Async XLA Ops:
  7.2 56.1 %all-gather.17.cloned.1.call-start = ((), (), s32[]{:S(2)}) async-start(), calls=%async_computation.19 | async-start | bytes 4386816 | tf_op jit(solution)/shard_map/all_gather | solution.py:67
  7.9 160.2 %all-gather.19.cloned.1.call-start = ((), (), s32[]{:S(2)}) async-start(), calls=%async_computation.20 | async-start | bytes 11943936 | tf_op jit(solution)/shard_map/all_gather | solution.py:73
  69.9 139.4 %all-gather.21.cloned.1.call-start = ((), (), s32[]{:S(2)}) async-start(), calls=%async_computation.21 | async-start | bytes 1566720 | tf_op jit(solution)/shard_map/all_gather | solution.py:68
  70.6 194.4 %all-gather.25.cloned.1.call-start = ((), (), s32[]{:S(2)}) async-start(), calls=%async_computation.23 | async-start | bytes 5326848 | tf_op jit(solution)/shard_map/all_gather | solution.py:69
  71.2 249.9 %all-gather.29.cloned.1.call-start = ((), (), s32[]{:S(2)}) async-start(), calls=%async_computation.25 | async-start | bytes 5326848 | tf_op jit(solution)/shard_map/all_gather | solution.py:70
  71.8 304.2 %all-gather.35.cloned.1.call-start = ((), (), s32[]{:S(2)}) async-start(), calls=%async_computation.29 | async-start | bytes 5013504 | tf_op jit(solution)/shard_map/all_gather | solution.py:116
  84.7 96.7 %copy-start.85 = (f32[1152]{0:T(1024)}, f32[1152]{0:T(1024)S(1)}, u32[]{:S(2)}) copy-start(f32[1152]{0:T(1024)S(1)} %mul.941) | copy-start | bytes 13828
  174.7 256.1 %all-gather.37.cloned.1.call-start = ((), (), s32[]{:S(2)}) async-start(), calls=%async_computation.30 | async-start | bytes 5013504 | tf_op jit(solution)/shard_map/all_gather | solution.py:116
  181.4 304.3 %all-gather.39.cloned.1.call-start = ((), (), s32[]{:S(2)}) async-start(), calls=%async_computation.31 | async-start | bytes 5013504 | tf_op jit(solution)/shard_map/all_gather | solution.py:116
  188.0 344.5 %all-gather.23.cloned.1.call-start = ((), (), s32[]{:S(2)}) async-start(), calls=%async_computation.22 | async-start | bytes 3981312 | tf_op jit(solution)/shard_map/all_gather | solution.py:74
  211.9 438.0 %all-gather.27.cloned.1.call-start = ((), (), s32[]{:S(2)}) async-start(), calls=%async_computation.24 | async-start | bytes 14874624 | tf_op jit(solution)/shard_map/all_gather | solution.py:75
  273.6 501.2 %all-gather.31.cloned.1.call-start = ((), (), s32[]{:S(2)}) async-start(), calls=%async_computation.26 | async-start | bytes 14874624 | tf_op jit(solution)/shard_map/all_gather | solution.py:76
  329.5 629.6 %reduce-scatter.62.cloned.1.call-start = ((), (), s32[]{:S(2)}) async-start(), calls=%async_computation.33 | async-start | bytes 5013504
  331.5 194.5 %copy-start.78 = (bf16[64,16,72]{2,1,0:T(8,128)(2,1)}, bf16[64,16,72]{2,1,0:T(8,128)(2,1)S(1)}, u32[]{:S(2)}) copy-start(bf16[64,16,72]{2,1,0:T(8,128)(2,1)S(1)} %reshape.1191) | copy-start | bytes 442372
  332.0 185.9 %copy-start.80 = (bf16[64,16,72]{2,1,0:T(8,128)(2,1)}, bf16[64,16,72]{2,1,0:T(8,128)(2,1)S(1)}, u32[]{:S(2)}) copy-start(bf16[64,16,72]{2,1,0:T(8,128)(2,1)S(1)} %reshape.1197) | copy-start | bytes 442372
  535.9 277.8 %copy-start.19 = (f32[64,1152]{1,0:T(8,128)}, f32[64,1152]{1,0:T(8,128)S(1)}, u32[]{:S(2)}) copy-start(f32[64,1152]{1,0:T(8,128)S(1)} %get-tuple-element.209) | copy-start | bytes 884740
  858.0 154.7 %reduce-scatter.66.cloned.1.call-start = ((), (), s32[]{:S(2)}) async-start(), calls=%async_computation.35 | async-start | bytes 5013504
  899.5 191.5 %reduce-scatter.64.cloned.1.call-start = ((), (), s32[]{:S(2)}) async-start(), calls=%async_computation.34 | async-start | bytes 5013504
  941.0 224.0 %all-gather.33.cloned.1.call-start = ((), (), s32[]{:S(2)}) async-start(), calls=%async_computation.28 | async-start | bytes 5013504 | tf_op jit(solution)/shard_map/all_gather | solution.py:116
  947.3 153.0 %copy-start.48 = (bf16[1,64,16,72]{1,3,2,0:T(8,128)(2,1)}, bf16[1,64,16,72]{1,3,2,0:T(8,128)(2,1)S(1)}, u32[]{:S(2)}) copy-start(bf16[1,64,16,72]{1,3,2,0:T(8,128)(2,1)S(1)} %copy.185) | copy-start | bytes 442372
  1112.4 229.1 %reduce-scatter.92.cloned.1.call-start = ((), (), s32[]{:S(2)}) async-start(), calls=%async_computation.49 | async-start | bytes 2820096
  1213.5 164.1 %reduce-scatter.60.cloned.1.call-start = ((), (), s32[]{:S(2)}) async-start(), calls=%async_computation.32 | async-start | bytes 5013504
  1253.6 169.4 %reduce-scatter.88.cloned.1.call-start = ((), (), s32[]{:S(2)}) async-start(), calls=%async_computation.46 | async-start | bytes 442368
  1255.3 233.4 %reduce-scatter.58.cloned.1.call-start = ((), (), s32[]{:S(2)}) async-start(), calls=%async_computation.27 | async-start | bytes 10653696 | tf_op jit(solution)/shard_map/reduce_scatter | solution.py:292
  1303.8 198.2 %reduce-scatter.86.cloned.1.call-start = ((), (), s32[]{:S(2)}) async-start(), calls=%async_computation.45 | async-start | bytes 442368
  1326.5 189.8 %reduce-scatter.78.cloned.1.call-start = ((), (), s32[]{:S(2)}) async-start(), calls=%async_computation.41 | async-start | bytes 442368
  1327.6 203.1 %reduce-scatter.80.cloned.1.call-start = ((), (), s32[]{:S(2)}) async-start(), calls=%async_computation.42 | async-start | bytes 442368
  1328.7 216.5 %reduce-scatter.70.cloned.1.call-start = ((), (), s32[]{:S(2)}) async-start(), calls=%async_computation.37 | async-start | bytes 442368
  1343.4 322.8 %reduce-scatter.72.cloned.1.call-start = ((), (), s32[]{:S(2)}) async-start(), calls=%async_computation.38 | async-start | bytes 10653696
  1371.6 399.1 %reduce-scatter.90.cloned.1.call-start = ((), (), s32[]{:S(2)}) async-start(), calls=%async_computation.48 | async-start | bytes 8460288
  1421.4 363.8 %reduce-scatter.74.cloned.1.call-start = ((), (), s32[]{:S(2)}) async-start(), calls=%async_computation.39 | async-start | bytes 442368
  1461.1 338.9 %reduce-scatter.76.cloned.1.call-start = ((), (), s32[]{:S(2)}) async-start(), calls=%async_computation.40 | async-start | bytes 442368
  1461.7 352.6 %reduce-scatter.84.cloned.1.call-start = ((), (), s32[]{:S(2)}) async-start(), calls=%async_computation.44 | async-start | bytes 442368
  1462.8 365.8 %reduce-scatter.82.cloned.1.call-start = ((), (), s32[]{:S(2)}) async-start(), calls=%async_computation.43 | async-start | bytes 442368
  1463.8 429.3 %all-reduce.24.cloned.1.call-start = ((), (), s32[]{:S(2)}) async-start(), calls=%async_computation.47 | async-start | bytes 1253376
  1488.7 406.3 %reduce-scatter.94.cloned.1.call-start = ((), (), s32[]{:S(2)}) async-start(), calls=%async_computation.50 | async-start | bytes 1652736
  1494.6 177.9 %copy-start.47 = (bf16[4,64,1152]{2,1,0:T(8,128)(2,1)S(1)}, bf16[4,64,1152]{2,1,0:T(8,128)(2,1)}, u32[]{:S(2)}) copy-start(bf16[4,64,1152]{2,1,0:T(8,128)(2,1)} %param.18) | copy-start | bytes 1769476
  1494.6 177.9 %copy-start.53 = (f32[64,1152]{1,0:T(8,128)S(1)}, f32[64,1152]{1,0:T(8,128)}, u32[]{:S(2)}) copy-start(f32[64,1152]{1,0:T(8,128)} %copy-done.51) | copy-start | bytes 884740
  1494.7 177.9 %copy-start.57 = (f32[64,1152]{1,0:T(8,128)S(1)}, f32[64,1152]{1,0:T(8,128)}, u32[]{:S(2)}) copy-start(f32[64,1152]{1,0:T(8,128)} %copy-done.55) | copy-start | bytes 884740
  1494.7 177.9 %copy-start.67 = (f32[64,1152]{1,0:T(8,128)S(1)}, f32[64,1152]{1,0:T(8,128)}, u32[]{:S(2)}) copy-start(f32[64,1152]{1,0:T(8,128)} %copy-done.66) | copy-start | bytes 884740
  1494.7 177.9 %copy-start.69 = (f32[64,1152]{1,0:T(8,128)S(1)}, f32[64,1152]{1,0:T(8,128)}, u32[]{:S(2)}) copy-start(f32[64,1152]{1,0:T(8,128)} %copy-done.68) | copy-start | bytes 884740
  1668.5 104.5 %copy-start.65 = (f32[64,1152]{1,0:T(8,128)S(1)}, f32[64,1152]{1,0:T(8,128)}, u32[]{:S(2)}) copy-start(f32[64,1152]{1,0:T(8,128)} %copy-done.64) | copy-start | bytes 884740
  1668.5 104.5 %copy-start.71 = (f32[64,1152]{1,0:T(8,128)S(1)}, f32[64,1152]{1,0:T(8,128)}, u32[]{:S(2)}) copy-start(f32[64,1152]{1,0:T(8,128)} %copy-done.70) | copy-start | bytes 884740
  1668.5 104.5 %copy-start.73 = (f32[64,1152]{1,0:T(8,128)S(1)}, f32[64,1152]{1,0:T(8,128)}, u32[]{:S(2)}) copy-start(f32[64,1152]{1,0:T(8,128)} %copy-done.72) | copy-start | bytes 884740
  1668.5 104.5 %copy-start.75 = (f32[64,1152]{1,0:T(8,128)S(1)}, f32[64,1152]{1,0:T(8,128)}, u32[]{:S(2)}) copy-start(f32[64,1152]{1,0:T(8,128)} %get-tuple-element.217) | copy-start | bytes 884740
  1668.5 237.8 %reduce-scatter.68.cloned.1.call-start = ((), (), s32[]{:S(2)}) async-start(), calls=%async_computation.36 | async-start | bytes 1327104
  1674.3 99.8 %copy-start.105 = (bf16[1,64,1152]{2,1,0:T(8,128)(2,1)S(1)}, bf16[1,64,1152]{2,1,0:T(8,128)(2,1)}, u32[]{:S(2)}) copy-start(bf16[1,64,1152]{2,1,0:T(8,128)(2,1)} %get-tuple-element.168) | copy-start | bytes 442372
  1674.3 99.8 %copy-start.106 = (bf16[1,64,1152]{2,1,0:T(8,128)(2,1)S(1)}, bf16[1,64,1152]{2,1,0:T(8,128)(2,1)}, u32[]{:S(2)}) copy-start(bf16[1,64,1152]{2,1,0:T(8,128)(2,1)} %get-tuple-element.169) | copy-start | bytes 442372
  (231 other events, 2464.1 us)
Sparse Core Ops, SparseCore 0:
  10.3 52.9 all-gather.16
  70.0 98.0 all-gather.18
  170.3 38.9 all-gather.20
  211.3 53.7 all-gather.24
  267.0 53.9 all-gather.28
  323.8 52.1 all-gather.34
  378.8 51.9 all-gather.36
  433.6 51.9 all-gather.38
  487.2 37.9 all-gather.22
  526.5 123.3 all-gather.26
  651.5 123.2 all-gather.30
  858.1 75.5 reduce-scatter.61
  938.0 74.6 reduce-scatter.65
  1016.4 74.5 reduce-scatter.63
  1112.6 52.4 all-gather.32
  1213.6 62.4 reduce-scatter.91
  1279.8 74.4 reduce-scatter.59
  1356.4 11.0 reduce-scatter.87
  1372.2 116.4 reduce-scatter.57
  1490.8 11.0 reduce-scatter.85
  1504.3 12.0 reduce-scatter.77
  1518.7 12.0 reduce-scatter.79
  1533.1 12.0 reduce-scatter.69
  1549.8 116.4 reduce-scatter.71
  1670.8 99.8 reduce-scatter.89
  1773.4 11.8 reduce-scatter.73
  1787.9 12.0 reduce-scatter.75
  1802.2 12.0 reduce-scatter.83
  1816.5 12.0 reduce-scatter.81
  1830.8 30.8 all-reduce.23
  1863.9 21.4 reduce-scatter.93
  1887.8 18.5 reduce-scatter.67
where the time goes:
time: 1930 us; the launch traced here: 1920 us
  waiting for transfers between devices  1090 us (56%)
  matrix products  339 us (18%)
  local copies, waits for them, and re-layouts  299 us (15%)
  blocking collectives  114 us (6%)
  other arithmetic  49.7 us (3%)
  between operations  20.6 us (1%)
    unnamed x51, waiting for transfers between devices  446 us
    unnamed x562, local copies, waits for them, and re-layouts  197 us
    all_gather x4, waiting for transfers between devices, per_device(): lax.all_gather(key_value, 'sa', axis=1, tiled=True)  189 us
    dot_general x16, matrix products, mat_rows(): lax.dot_general(left, right, (((0,), (0,)), ((), ())), preferred_element_...  140 us
    all_gather x1, waiting for transfers between devices, per_device(): lax.all_gather(row_parts[3], 'dev', axis=1, tiled=True)  108 us
    all_gather x1, waiting for transfers between devices, per_device(): lax.all_gather(row_parts[2], 'dev', axis=1, tiled=True)  106 us
    all_gather x1, waiting for transfers between devices, per_device(): lax.all_gather(row_parts[0], 'dev', axis=1, tiled=True)  82.3 us
    psum x1, blocking collectives, per_device(): lax.psum((column_sums[4], column_sums[5], column_sums[6], column_sums[7],...  63.4 us
  transfers between devices with their start and end apart: 32, of which 25 were waited for; matrix products, arithmetic and copies ran while one was open for 27% of the time, Pallas kernels for 0%

commit v1 on v0

--- a/solution.py
+++ b/solution.py
@@ -6,6 +6,18 @@
 HEADS = 16
 HEAD_DIM = 72
 MICRO = 4
+
+
+def collect(x, axis, dim):
+    ways, here = (lax.axis_size(axis), lax.axis_index(axis))
+    grown, reach = (x, 1)
+    while reach < ways:
+        theirs = lax.ppermute(grown, axis, [(d, d ^ reach) for d in range(ways)])
+        mine_first = jnp.concatenate([grown, theirs], axis=dim)
+        theirs_first = jnp.concatenate([theirs, grown], axis=dim)
+        grown = jnp.where(here & reach == 0, mine_first, theirs_first)
+        reach = 2 * reach
+    return grown
 
 
 def normalize(values, gain, shift):
@@ -64,7 +76,7 @@
     row_count = per_micro * local_tokens
     scale = HEAD_DIM ** (-0.5)
     row_parts = (
-        lax.all_gather(w_qkv, "sa", axis=0, tiled=True),
+        collect(w_qkv, "sa", 0),
         lax.all_gather(w_out, "sa", axis=0, tiled=True),
         lax.all_gather(w_up, "sa", axis=0, tiled=True),
         lax.all_gather(w_down, "sa", axis=0, tiled=True),

time: 1930 us -> 2110 us (1.093)
  waiting for transfers between devices: 1090 us -> 1260 us
    ppermute x0 -> x4, waiting for transfers between devices: none -> 124 us  [collect(): theirs = lax.ppermute(grown, axis, [(d, d ^ reach) for d in range(ways)])]
    all_gather x0 -> x1, waiting for transfers between devices: none -> 95.6 us  [per_device(): lax.all_gather(rows_back[0], 'dev', axis=1, tiled=True)]
    all_gather x1, waiting for transfers between devices: 55.3 us -> 0.02 us  [per_device(): lax.all_gather(w_qkv, 'sa', axis=0, tiled=True)]
    all_gather x4, waiting for transfers between devices: 189 us -> 142 us  [per_device(): lax.all_gather(key_value, 'sa', axis=1, tiled=True)]
    all_gather x1, waiting for transfers between devices: 10.2 us -> 47 us  [per_device(): lax.all_gather(w_down, 'sa', axis=0, tiled=True)]
    unnamed x51 -> x52, waiting for transfers between devices: 446 us -> 440 us
    unnamed x562 -> x552, local copies, waits for them, and re-layouts: 197 us -> 199 us
  transfers between devices with their start and end apart: 32 -> 37, of which waited for: 25 -> 30; matrix products, arithmetic and copies ran while one was open for 27% -> 29% of each run, Pallas kernels for 0% -> 0%
where the time goes in v1:
time: 2110 us; the launch traced here: 2100 us
  waiting for transfers between devices  1260 us (60%)
  matrix products  330 us (16%)
  local copies, waits for them, and re-layouts  309 us (15%)
  blocking collectives  113 us (5%)
  other arithmetic  57.4 us (3%)
    unnamed x52, waiting for transfers between devices  440 us
    unnamed x552, local copies, waits for them, and re-layouts  199 us
    all_gather x4, waiting for transfers between devices, per_device(): lax.all_gather(key_value, 'sa', axis=1, tiled=True)  142 us
    dot_general x16, matrix products, mat_rows(): lax.dot_general(left, right, (((0,), (0,)), ((), ())), preferred_element_...  141 us
    ppermute x4, waiting for transfers between devices, collect(): theirs = lax.ppermute(grown, axis, [(d, d ^ reach) for d in range(ways)])  124 us
    all_gather x1, waiting for transfers between devices, per_device(): lax.all_gather(row_parts[3], 'dev', axis=1, tiled=True)  117 us
    all_gather x1, waiting for transfers between devices, per_device(): lax.all_gather(rows_back[0], 'dev', axis=1, tiled=True)  95.6 us
    all_gather x1, waiting for transfers between devices, per_device(): lax.all_gather(row_parts[2], 'dev', axis=1, tiled=True)  94.9 us
  transfers between devices with their start and end apart: 37, of which 30 were waited for; matrix products, arithmetic and copies ran while one was open for 29% of the time, Pallas kernels for 0%

profile of v1, /device:TPU:0, one launch (start us, length us, event | category | flops | bytes accessed | tf_op | source)
XLA Modules:
  0.0 2096.6 jit_solution(8159988051339093203)
XLA Ops:
  13.3 12.0 collective-permute-done.1
  27.4 22.6 %collective-permute-done.2 = bf16[288,1728]{1,0:T(8,128)(2,1)} collective-permute-done((bf16[288,1728]{1,0:T(8,128)(2,1)S(1)}, bf16[288,1728]{1,0:T(8,128)(2,1)}, u32[]{:S(2)}, u32[]{:S(2)}) %collective-permute-start.2) | collective-permute-done | bytes 995360 | tf_op jit(solution)/shard_map/ppermute | solution.py:15
  54.9 88.3 %collective-permute-done.3 = bf16[576,1728]{1,0:T(8,128)(2,1)} collective-permute-done((bf16[576,1728]{1,0:T(8,128)(2,1)S(1)}, bf16[576,1728]{1,0:T(8,128)(2,1)}, u32[]{:S(2)}, u32[]{:S(2)}) %collective-permute-start.3) | collective-permute-done | bytes 1990688 | tf_op jit(solution)/shard_map/ppermute | solution.py:15
  169.6 84.8 %all-gather.18.cloned.1.call-done = bf16[1152,3456]{0,1:T(8,128)(2,1)} async-done(((bf16[1152,1728]{0,1:T(8,128)(2,1)}), bf16[1152,3456]{0,1:T(8,128)(2,1)}) %all-gather.18.cloned.1.call-update) | async-done | bytes 7962640 | tf_op jit(solution)/shard_map/all_gather | solution.py:85
  260.9 34.9 %all-gather.20.cloned.1.call-done = bf16[1152,576]{1,0:T(8,128)(2,1)} async-done(((bf16[72,576]{1,0:T(8,128)(2,1)}), bf16[1152,576]{1,0:T(8,128)(2,1)}) %all-gather.20.cloned.1.call-update) | async-done | bytes 1327120 | tf_op jit(solution)/shard_map/all_gather | solution.py:80
  311.8 40.0 %all-gather.24.cloned.1.call-done = bf16[1152,2152]{1,0:T(8,128)(2,1)} async-done(((bf16[72,2152]{1,0:T(8,128)(2,1)}), bf16[1152,2152]{1,0:T(8,128)(2,1)}) %all-gather.24.cloned.1.call-update) | async-done | bytes 4958224 | tf_op jit(solution)/shard_map/all_gather | solution.py:81
  351.8 8.4 copy.151
  360.3 47.0 %all-gather.28.cloned.1.call-done = bf16[1152,2152]{1,0:T(8,128)(2,1)} async-done(((bf16[72,2152]{1,0:T(8,128)(2,1)}), bf16[1152,2152]{1,0:T(8,128)(2,1)}) %all-gather.28.cloned.1.call-update) | async-done | bytes 4958224 | tf_op jit(solution)/shard_map/all_gather | solution.py:82
  419.3 32.9 %all-reduce.19 = (bf16[1024]{0:T(1024)(128)(2,1)S(1)}, bf16[1024]{0:T(1024)(128)(2,1)S(1)}, bf16[1024]{0:T(1024)(128)(2,1)S(1)}, bf16[1024]{0:T(1024)(128)(2,1)S(1)}) all-reduce(bf16[1024]{0:T(1024)(128)(2,1)S(1)} %dynamic-update-slice.10, bf16[1024]{0:T(1024)(128)(2,1)S(1)} %dynamic-update-slice.12, ...), channel_id=1, replica_groups=mesh['dev'=2,'sa'=16] {'sa'}, use_global_device_ids=true, to_apply=%add.10 | all-reduce | flops 4096 | bytes 16384
  481.1 20.8 all-gather.22.cloned.1.call-done
  506.1 52.1 %all-gather.40.cloned.1.call-done = bf16[1024,2304]{1,0:T(8,128)(2,1)} async-done(((bf16[64,2304]{1,0:T(8,128)(2,1)}), bf16[1024,2304]{1,0:T(8,128)(2,1)}) %all-gather.40.cloned.1.call-update) | async-done | bytes 4718608 | tf_op jit(solution)/shard_map/all_gather | solution.py:128
  580.9 32.1 %all-gather.42.cloned.1.call-done = bf16[1024,2304]{1,0:T(8,128)(2,1)} async-done(((bf16[64,2304]{1,0:T(8,128)(2,1)}), bf16[1024,2304]{1,0:T(8,128)(2,1)}) %all-gather.42.cloned.1.call-update) | async-done | bytes 4718608 | tf_op jit(solution)/shard_map/all_gather | solution.py:128
  641.6 94.9 %all-gather.26.cloned.1.call-done = bf16[1152,4304]{0,1:T(8,128)(2,1)} async-done(((bf16[1152,2152]{0,1:T(8,128)(2,1)}), bf16[1152,4304]{0,1:T(8,128)(2,1)}) %all-gather.26.cloned.1.call-update) | async-done | bytes 9916432 | tf_op jit(solution)/shard_map/all_gather | solution.py:87
  744.3 116.9 %all-gather.30.cloned.1.call-done = bf16[1152,4304]{0,1:T(8,128)(2,1)} async-done(((bf16[1152,2152]{0,1:T(8,128)(2,1)}), bf16[1152,4304]{0,1:T(8,128)(2,1)}) %all-gather.30.cloned.1.call-update) | async-done | bytes 9916432 | tf_op jit(solution)/shard_map/all_gather | solution.py:88
  916.3 21.3 %copy.193 = bf16[1,1024,2304]{2,0,1:T(2,128)(2,1)} copy(bf16[1,1024,2304]{1,2,0:T(8,128)(2,1)} %pad_maximum_fusion.1) | data formatting | bytes 9437184
  957.7 21.5 %copy.195 = bf16[1,1024,2304]{2,0,1:T(2,128)(2,1)} copy(bf16[1,1024,2304]{1,2,0:T(8,128)(2,1)} %pad_maximum_fusion.2) | data formatting | bytes 9437184
  999.2 21.8 %copy.197 = bf16[1,1024,2304]{2,0,1:T(2,128)(2,1)} copy(bf16[1,1024,2304]{1,2,0:T(8,128)(2,1)} %pad_maximum_fusion.3) | data formatting | bytes 9437184
  1056.1 43.0 %reduce-scatter.64.cloned.1.call-done = bf16[64,2304]{1,0:T(8,128)(2,1)} async-done(((bf16[1024,2304]{1,0:T(8,128)(2,1)}), bf16[64,2304]{1,0:T(8,128)(2,1)}) %reduce-scatter.64.cloned.1.call-update) | async-done | bytes 294928
  1103.3 74.1 %reduce-scatter.66.cloned.1.call-done = bf16[64,2304]{1,0:T(8,128)(2,1)} async-done(((bf16[1024,2304]{1,0:T(8,128)(2,1)}), bf16[64,2304]{1,0:T(8,128)(2,1)}) %reduce-scatter.66.cloned.1.call-update) | async-done | bytes 294928
  1181.6 95.6 %all-gather.34.cloned.1.call-done = bf16[1152,3456]{0,1:T(8,128)(2,1)} async-done(((bf16[1152,1728]{0,1:T(8,128)(2,1)}), bf16[1152,3456]{0,1:T(8,128)(2,1)}) %all-gather.34.cloned.1.call-update) | async-done | bytes 7962640 | tf_op jit(solution)/shard_map/all_gather | solution.py:175
  1295.3 50.5 %all-gather.36.cloned.1.call-done = bf16[1024,2304]{1,0:T(8,128)(2,1)} async-done(((bf16[64,2304]{1,0:T(8,128)(2,1)}), bf16[1024,2304]{1,0:T(8,128)(2,1)}) %all-gather.36.cloned.1.call-update) | async-done | bytes 4718608 | tf_op jit(solution)/shard_map/all_gather | solution.py:128
  1406.2 21.6 %copy.191 = bf16[1,1024,2304]{2,0,1:T(2,128)(2,1)} copy(bf16[1,1024,2304]{1,2,0:T(8,128)(2,1)} %pad_maximum_fusion) | data formatting | bytes 9437184
  1436.3 8.6 fusion.245
  1445.0 13.0 convolution_add_fusion.5
  1458.1 13.4 convolution_add_fusion.4
  1471.5 13.5 fusion
  1486.7 8.4 fusion.201
  1495.1 12.7 convolution_add_fusion.2
  1510.1 12.9 convolution_add_fusion.1
  1524.9 14.0 fusion.2
  1538.8 14.1 copy.205
  1562.6 11.0 fusion.156
  1573.6 8.7 convolution_add_fusion.8
  1582.4 8.5 convolution_add_fusion.7
  1590.9 11.1 fusion.3
  1614.0 9.0 all-reduce.20
  1654.4 15.1 reduce-scatter.58.cloned.1.call-done
  1684.6 12.8 reduce-scatter.78.cloned.1.call-done
  1699.0 12.8 reduce-scatter.80.cloned.1.call-done
  1713.4 12.6 reduce-scatter.70.cloned.1.call-done
  1727.8 119.4 %reduce-scatter.72.cloned.1.call-done = bf16[72,4304]{1,0:T(8,128)(2,1)} async-done(((bf16[1152,4304]{1,0:T(8,128)(2,1)}), bf16[72,4304]{1,0:T(8,128)(2,1)}) %reduce-scatter.72.cloned.1.call-update) | async-done | bytes 619792
  1855.4 96.2 %reduce-scatter.90.cloned.1.call-done = bf16[72,3456]{1,0:T(8,128)(2,1)} async-done(((bf16[1152,3456]{1,0:T(8,128)(2,1)}), bf16[72,3456]{1,0:T(8,128)(2,1)}) %reduce-scatter.90.cloned.1.call-update) | async-done | bytes 497680
  1955.9 9.6 reduce-scatter.82.cloned.1.call-done
  1966.6 13.3 reduce-scatter.84.cloned.1.call-done
  1980.9 13.9 reduce-scatter.76.cloned.1.call-done
  1995.8 13.7 reduce-scatter.74.cloned.1.call-done
  2010.6 63.4 %all-reduce.18 = (f32[1,576]{1,0:T(1,128)}, f32[1,576]{1,0:T(1,128)}, f32[1,576]{1,0:T(1,128)}, f32[1,576]{1,0:T(1,128)}, f32[1,576]{1,0:T(1,128)}, /*index=5*/f...) all-reduce(bf16[1,576]{1,0:T(2,128)(2,1)S(1)} %copy.208, ...), channel_id=1, replica_groups=mesh['dev'=2,'sa'=16] {'sa'}, use_global_device_ids=true, to_apply=%region_61.62 | all-reduce | flops 6760 | bytes 44864 | tf_op jit(solution)/shard_map/psum | solution.py:353
  2078.1 9.2 reduce-scatter.68.cloned.1.call-done
  (841 shorter events, 487.6 us)
Async XLA Ops:
  7.2 247.1 %all-gather.18.cloned.1.call-start = ((), (), s32[]{:S(2)}) async-start(), calls=%async_computation.19 | async-start | bytes 11943936 | tf_op jit(solution)/shard_map/all_gather | solution.py:85
  7.2 1.9 collective-permute-start
  10.3 15.0 collective-permute-start.1
  25.6 24.5 %collective-permute-start.2 = (bf16[288,1728]{1,0:T(8,128)(2,1)S(1)}, bf16[288,1728]{1,0:T(8,128)(2,1)}, u32[]{:S(2)}, u32[]{:S(2)}) collective-permute-start(bf16[288,1728]{1,0:T(8,128)(2,1)S(1)} %maximum_select_fusion.2), channel_id=1, source_target_pairs={{0,4},{1,5},{2,6},{3,7},{4,0},{5,1},{6,2},{7,3},{8,12},{9,13},{10,... | collective-permute-start | bytes 2985992 | tf_op jit(solution)/shard_map/ppermute | solution.py:15
  52.3 90.9 %collective-permute-start.3 = (bf16[576,1728]{1,0:T(8,128)(2,1)S(1)}, bf16[576,1728]{1,0:T(8,128)(2,1)}, u32[]{:S(2)}, u32[]{:S(2)}) collective-permute-start(bf16[576,1728]{1,0:T(8,128)(2,1)S(1)} %maximum_select_fusion.1), channel_id=1, source_target_pairs={{0,8},{1,9},{2,10},{3,11},{4,12},{5,13},{6,14},{7,15},{8,0},{9,1},... | collective-permute-start | bytes 5971976 | tf_op jit(solution)/shard_map/ppermute | solution.py:15
  154.2 141.6 %all-gather.20.cloned.1.call-start = ((), (), s32[]{:S(2)}) async-start(), calls=%async_computation.20 | async-start | bytes 1566720 | tf_op jit(solution)/shard_map/all_gather | solution.py:80
  155.0 196.8 %all-gather.24.cloned.1.call-start = ((), (), s32[]{:S(2)}) async-start(), calls=%async_computation.22 | async-start | bytes 5326848 | tf_op jit(solution)/shard_map/all_gather | solution.py:81
  155.7 251.6 %all-gather.28.cloned.1.call-start = ((), (), s32[]{:S(2)}) async-start(), calls=%async_computation.24 | async-start | bytes 5326848 | tf_op jit(solution)/shard_map/all_gather | solution.py:82
  156.3 306.2 %all-gather.38.cloned.1.call-start = ((), (), s32[]{:S(2)}) async-start(), calls=%async_computation.30 | async-start | bytes 5013504 | tf_op jit(solution)/shard_map/all_gather | solution.py:128
  168.5 136.7 %copy-start.89 = (f32[1152]{0:T(1024)}, f32[1152]{0:T(1024)S(1)}, u32[]{:S(2)}) copy-start(f32[1152]{0:T(1024)S(1)} %mul.941) | copy-start | bytes 13828
  168.5 136.7 %copy-start.106 = (f32[1152]{0:T(1024)}, f32[1152]{0:T(1024)S(1)}, u32[]{:S(2)}) copy-start(f32[1152]{0:T(1024)S(1)} %add.879) | copy-start | bytes 13828
  168.5 136.7 %copy-start.115 = (f32[3456]{0:T(1024)}, f32[3456]{0:T(1024)S(1)}, u32[]{:S(2)}) copy-start(f32[3456]{0:T(1024)S(1)} %pad_maximum_fusion.18) | copy-start | bytes 41476
  169.2 136.0 %copy-start.156 = (f32[64]{0:T(128)}, f32[64]{0:T(128)S(1)}, u32[]{:S(2)}) copy-start(f32[64]{0:T(128)S(1)} %get-tuple-element.230) | copy-start | bytes 772
  260.9 241.1 %all-gather.22.cloned.1.call-start = ((), (), s32[]{:S(2)}) async-start(), calls=%async_computation.21 | async-start | bytes 3981312 | tf_op jit(solution)/shard_map/all_gather | solution.py:86
  298.5 259.7 %all-gather.40.cloned.1.call-start = ((), (), s32[]{:S(2)}) async-start(), calls=%async_computation.31 | async-start | bytes 5013504 | tf_op jit(solution)/shard_map/all_gather | solution.py:128
  305.1 308.0 %all-gather.42.cloned.1.call-start = ((), (), s32[]{:S(2)}) async-start(), calls=%async_computation.32 | async-start | bytes 5013504 | tf_op jit(solution)/shard_map/all_gather | solution.py:128
  311.8 424.7 %all-gather.26.cloned.1.call-start = ((), (), s32[]{:S(2)}) async-start(), calls=%async_computation.23 | async-start | bytes 14874624 | tf_op jit(solution)/shard_map/all_gather | solution.py:87
  360.2 501.0 %all-gather.30.cloned.1.call-start = ((), (), s32[]{:S(2)}) async-start(), calls=%async_computation.25 | async-start | bytes 14874624 | tf_op jit(solution)/shard_map/all_gather | solution.py:88
  415.7 611.9 %all-gather.32.cloned.1.call-start = ((), (), s32[]{:S(2)}) async-start(), calls=%async_computation.26 | async-start | bytes 4386816 | tf_op jit(solution)/shard_map/all_gather | solution.py:169
  416.5 635.5 %reduce-scatter.62.cloned.1.call-start = ((), (), s32[]{:S(2)}) async-start(), calls=%async_computation.34 | async-start | bytes 5013504
  579.1 320.9 %copy-start.21 = (f32[64,1152]{1,0:T(8,128)}, f32[64,1152]{1,0:T(8,128)S(1)}, u32[]{:S(2)}) copy-start(f32[64,1152]{1,0:T(8,128)S(1)} %get-tuple-element.203) | copy-start | bytes 884740
  944.3 154.9 %reduce-scatter.64.cloned.1.call-start = ((), (), s32[]{:S(2)}) async-start(), calls=%async_computation.35 | async-start | bytes 5013504
  985.8 191.6 %reduce-scatter.66.cloned.1.call-start = ((), (), s32[]{:S(2)}) async-start(), calls=%async_computation.36 | async-start | bytes 5013504
  1027.6 249.6 %all-gather.34.cloned.1.call-start = ((), (), s32[]{:S(2)}) async-start(), calls=%async_computation.27 | async-start | bytes 11943936 | tf_op jit(solution)/shard_map/all_gather | solution.py:175
  1034.1 311.7 %all-gather.36.cloned.1.call-start = ((), (), s32[]{:S(2)}) async-start(), calls=%async_computation.29 | async-start | bytes 5013504 | tf_op jit(solution)/shard_map/all_gather | solution.py:128
  1040.5 244.1 %copy-start.51 = (bf16[1,64,16,72]{1,3,2,0:T(8,128)(2,1)}, bf16[1,64,16,72]{1,3,2,0:T(8,128)(2,1)S(1)}, u32[]{:S(2)}) copy-start(bf16[1,64,16,72]{1,3,2,0:T(8,128)(2,1)S(1)} %copy.188) | copy-start | bytes 442372
  1292.3 230.7 %reduce-scatter.92.cloned.1.call-start = ((), (), s32[]{:S(2)}) async-start(), calls=%async_computation.50 | async-start | bytes 2820096
  1394.4 163.9 %reduce-scatter.60.cloned.1.call-start = ((), (), s32[]{:S(2)}) async-start(), calls=%async_computation.33 | async-start | bytes 5013504
  1434.6 169.0 %reduce-scatter.88.cloned.1.call-start = ((), (), s32[]{:S(2)}) async-start(), calls=%async_computation.47 | async-start | bytes 442368
  1436.3 233.2 %reduce-scatter.58.cloned.1.call-start = ((), (), s32[]{:S(2)}) async-start(), calls=%async_computation.28 | async-start | bytes 10653696 | tf_op jit(solution)/shard_map/reduce_scatter | solution.py:304
  1485.0 198.0 %reduce-scatter.86.cloned.1.call-start = ((), (), s32[]{:S(2)}) async-start(), calls=%async_computation.46 | async-start | bytes 442368
  1507.9 189.5 %reduce-scatter.78.cloned.1.call-start = ((), (), s32[]{:S(2)}) async-start(), calls=%async_computation.42 | async-start | bytes 442368
  1509.0 202.9 %reduce-scatter.80.cloned.1.call-start = ((), (), s32[]{:S(2)}) async-start(), calls=%async_computation.43 | async-start | bytes 442368
  1510.0 216.0 %reduce-scatter.70.cloned.1.call-start = ((), (), s32[]{:S(2)}) async-start(), calls=%async_computation.38 | async-start | bytes 442368
  1524.8 322.4 %reduce-scatter.72.cloned.1.call-start = ((), (), s32[]{:S(2)}) async-start(), calls=%async_computation.39 | async-start | bytes 10653696
  1553.0 398.7 %reduce-scatter.90.cloned.1.call-start = ((), (), s32[]{:S(2)}) async-start(), calls=%async_computation.49 | async-start | bytes 8460288
  1602.1 363.5 %reduce-scatter.82.cloned.1.call-start = ((), (), s32[]{:S(2)}) async-start(), calls=%async_computation.44 | async-start | bytes 442368
  1638.9 341.0 %reduce-scatter.84.cloned.1.call-start = ((), (), s32[]{:S(2)}) async-start(), calls=%async_computation.45 | async-start | bytes 442368
  1644.9 349.9 %reduce-scatter.76.cloned.1.call-start = ((), (), s32[]{:S(2)}) async-start(), calls=%async_computation.41 | async-start | bytes 442368
  1646.9 362.6 %reduce-scatter.74.cloned.1.call-start = ((), (), s32[]{:S(2)}) async-start(), calls=%async_computation.40 | async-start | bytes 442368
  1647.9 426.0 %all-reduce.24.cloned.1.call-start = ((), (), s32[]{:S(2)}) async-start(), calls=%async_computation.48 | async-start | bytes 1253376
  1669.6 406.4 %reduce-scatter.94.cloned.1.call-start = ((), (), s32[]{:S(2)}) async-start(), calls=%async_computation.51 | async-start | bytes 1652736
  1675.5 178.2 %copy-start.50 = (bf16[4,64,1152]{2,1,0:T(8,128)(2,1)S(1)}, bf16[4,64,1152]{2,1,0:T(8,128)(2,1)}, u32[]{:S(2)}) copy-start(bf16[4,64,1152]{2,1,0:T(8,128)(2,1)} %param.18) | copy-start | bytes 1769476
  1675.5 178.2 %copy-start.74 = (f32[64,1152]{1,0:T(8,128)S(1)}, f32[64,1152]{1,0:T(8,128)}, u32[]{:S(2)}) copy-start(f32[64,1152]{1,0:T(8,128)} %copy-done.73) | copy-start | bytes 884740
  1675.5 178.2 %copy-start.76 = (f32[64,1152]{1,0:T(8,128)S(1)}, f32[64,1152]{1,0:T(8,128)}, u32[]{:S(2)}) copy-start(f32[64,1152]{1,0:T(8,128)} %copy-done.75) | copy-start | bytes 884740
  1675.5 178.2 %copy-start.78 = (f32[64,1152]{1,0:T(8,128)S(1)}, f32[64,1152]{1,0:T(8,128)}, u32[]{:S(2)}) copy-start(f32[64,1152]{1,0:T(8,128)} %copy-done.77) | copy-start | bytes 884740
  1675.5 178.2 %copy-start.79 = (f32[64,1152]{1,0:T(8,128)S(1)}, f32[64,1152]{1,0:T(8,128)}, u32[]{:S(2)}) copy-start(f32[64,1152]{1,0:T(8,128)} %get-tuple-element.217) | copy-start | bytes 884740
  1849.6 237.7 %reduce-scatter.68.cloned.1.call-start = ((), (), s32[]{:S(2)}) async-start(), calls=%async_computation.37 | async-start | bytes 1327104
  (231 other events, 3223.6 us)
Sparse Core Ops, SparseCore 0:
  154.4 99.9 all-gather.17
  256.5 39.3 all-gather.19
  298.0 53.7 all-gather.23
  353.8 53.4 all-gather.27
  410.0 52.4 all-gather.37
  463.9 37.9 all-gather.21
  504.8 53.3 all-gather.39
  561.1 51.9 all-gather.41
  614.6 121.7 all-gather.25
  737.9 123.2 all-gather.29
  863.5 50.1 all-gather.31
  944.4 75.7 reduce-scatter.61
  1024.5 74.5 reduce-scatter.63
  1102.8 74.5 reduce-scatter.65
  1178.9 98.2 all-gather.33
  1292.4 53.3 all-gather.35
  1394.5 62.4 reduce-scatter.91
  1460.6 74.3 reduce-scatter.59
  1537.4 11.0 reduce-scatter.87
  1553.1 116.3 reduce-scatter.57
  1671.8 11.1 reduce-scatter.85
  1685.4 12.0 reduce-scatter.77
  1699.8 12.0 reduce-scatter.79
  1714.0 12.0 reduce-scatter.69
  1730.8 116.3 reduce-scatter.71
  1851.7 99.8 reduce-scatter.89
  1953.7 11.8 reduce-scatter.81
  1967.8 12.0 reduce-scatter.83
  1982.7 12.0 reduce-scatter.75
  1997.4 12.0 reduce-scatter.73
  2011.8 30.8 all-reduce.23
  2045.0 21.4 reduce-scatter.93
  2068.7 18.5 reduce-scatter.67
